TPU v7x, 32 devices: a whole 2x2x4 slice. The times are simulated.
32 devices in a mesh: dp: 4 (over z), ctx: 2 (over core), tp: 4 (over y, x).
Axes of the slice: x: 2, y: 2, z: 4, core: 2. Of those that a mesh axis runs over, the one named last changes fastest.
Arguments:
- block_in: bfloat16 [8192, 2048], P(('dp', 'ctx')), may hold values from -6 to 6
- query_proj: bfloat16 [2048, 2048], P('dp', 'tp'), may hold values from -0.125 to 0.125
- forget_proj: bfloat16 [2048, 2048], P('dp', 'tp'), may hold values from -0.0625 to 0.0625
- value_proj: bfloat16 [2048, 2048], P('dp', 'tp'), may hold values from -0.125 to 0.125
- outgate_proj: bfloat16 [2048, 2048], P('dp', 'tp'), may hold values from -0.125 to 0.125
- out_proj: bfloat16 [2048, 2048], P('tp', 'dp'), may hold values from -0.125 to 0.125
- ffn_gate: bfloat16 [2048, 5632], P('dp', 'tp'), may hold values from -0.125 to 0.125
- ffn_up: bfloat16 [2048, 5632], P('dp', 'tp'), may hold values from -0.125 to 0.125
- ffn_down: bfloat16 [5632, 2048], P('tp', 'dp'), may hold values from -0.078125 to 0.078125
- first_gain: float32 [2048], replicated, may hold values from 0.5 to 1.5
- second_gain: float32 [2048], replicated, may hold values from 0.5 to 1.5
- group_gain: float32 [2048], P('tp'), may hold values from 0.5 to 1.5
- forget_bias: float32 [2048], P('tp'), may hold values from 3 to 12
- bound_table: float32 [24, 2048], P(None, 'tp'), may hold values from -4 to 4
- layer_index: int32 [1], replicated, may hold values from 1 to 23
- second_start: int32 [4], P('dp'), may hold values from 1 to 2048, as said below
- cotangent: bfloat16 [8192, 2048], P(('dp', 'ctx')), may hold values from -6 to 6
Outputs:
- block_out: bfloat16 [8192, 2048], P(('dp', 'ctx'))
- input_grad: float32 [8192, 2048], P(('dp', 'ctx'))
- query_grad: float32 [2048, 2048], P('dp', 'tp')
- forget_grad: float32 [2048, 2048], P('dp', 'tp')
- value_grad: float32 [2048, 2048], P('dp', 'tp')
- outgate_grad: float32 [2048, 2048], P('dp', 'tp')
- out_proj_grad: float32 [2048, 2048], P('tp', 'dp')
- ffn_gate_grad: float32 [2048, 5632], P('dp', 'tp')
- ffn_up_grad: float32 [2048, 5632], P('dp', 'tp')
- ffn_down_grad: float32 [5632, 2048], P('tp', 'dp')
- first_gain_grad: float32 [2048], replicated
- second_gain_grad: float32 [2048], replicated
- group_gain_grad: float32 [2048], P('tp')
- forget_bias_grad: float32 [2048], P('tp')
- bound_table_grad: float32 [24, 2048], P(None, 'tp')
Inputs may be any that keep to these rules, and one draw needn't show every extreme that they name: second_start[p] is 2048 where pack p is one whole sequence, and otherwise the position inside the pack where its second sequence begins; pack 0 is always one whole sequence and pack 1 always holds two. layer_index names a row of bound_table other than the first.
All inputs are finite; a program needn't handle non-finite values.
Results may differ from a plain program's by a relative error of at most 0.018.
Values may be sent and summed in bfloat16 or wider, within the bound.
No kernel may reach another device: no remote copies, remote signals or barrier semaphores. Data moves between devices by JAX's collectives and lax.ppermute only.
A program may use at most 384 MiB of HBM per device.

v0:
```python
import jax
import jax.numpy as jnp
from jax import lax
from jax.sharding import PartitionSpec as P

HEAD = 128
BLOCK = 32
HIGH = lax.Precision.HIGHEST
EPS_NORM = 1e-06
EPS_GROUP = 1e-05


def carried_in(value, axis, join, neutral):
    count, mine = (lax.axis_size(axis), lax.axis_index(axis))
    pieces = jax.tree.map(lambda part: lax.all_gather(part, axis), value)
    total = jax.tree.map(
        lambda part, zero: jnp.full_like(part, 0) + jnp.asarray(zero, part.dtype), value, neutral
    )

    def hop(position, total):
        longer = join(total, jax.tree.map(lambda part: part[position], pieces))
        return jax.tree.map(lambda new, old: jnp.where(position < mine, new, old), longer, total)

    return lax.fori_loop(0, count - 1, hop, total)


def carried_in_2(array, axis, combine, identity):
    peers, index = (lax.axis_size(axis), lax.axis_index(axis))
    everything = jax.tree.map(
        lambda part, kind: lax.all_gather(part.astype(kind), axis),
        array,
        jax.tree.map(lambda a: jnp.bfloat16 if a.dtype == jnp.float32 else a.dtype, array),
    )
    start = jax.tree.map(
        lambda part, zero: jnp.broadcast_to(jnp.asarray(zero, part.dtype), part.shape),
        array,
        identity,
    )

    def hop(k, before):
        at = peers - 1 - k
        reached = at > index
        new = combine(
            before, jax.tree.map(lambda part, own: part[at].astype(own.dtype), everything, array)
        )
        return jax.tree.map(lambda a, b: jnp.where(reached, a, b), new, before)

    return lax.fori_loop(0, peers, hop, start)


def rms_norm(rows_in, gain_vec):
    return (
        rows_in
        * lax.rsqrt(jnp.mean(rows_in * rows_in, axis=-1, keepdims=True) + EPS_NORM)
        * gain_vec
    )


def head_norm(mixed, pre_gate, gain_vec, head_count):
    row_count = mixed.shape[0]
    grouped = mixed.reshape(row_count, head_count, -1)
    scaled = grouped * lax.rsqrt(jnp.mean(grouped * grouped, axis=-1, keepdims=True) + EPS_GROUP)
    return scaled.reshape(row_count, -1) * gain_vec * jax.nn.silu(pre_gate)


def lower_bound(bound_rows, which_layer):
    weights = jax.nn.softmax(bound_rows, axis=0)
    rising = jnp.cumsum(weights, axis=0) - weights[0:1]
    picked = (
        lax.broadcasted_iota(jnp.int32, (bound_rows.shape[0], 1), 0) == which_layer[0]
    ).astype(bound_rows.dtype)
    return jnp.sum(rising * picked, axis=0)


def gate_values(pre_query, pre_forget, bias_vec, bound_vec):
    shifted = pre_forget + bias_vec
    forget = bound_vec + (1.0 - bound_vec) * jax.nn.sigmoid(shifted)
    return (jax.nn.silu(pre_query), (1.0 - bound_vec) * jax.nn.sigmoid(-shifted), jnp.log(forget))


def chain_link(earlier, later):
    return (earlier[0] * later[0], later[0][..., None] * earlier[1] + later[1])


def contract_last(left_side, right_side):
    return lax.dot_general(
        left_side, right_side, (((1,), (1,)), ((), ())), preferred_element_type=jnp.float32
    )


def contract_first(left_side, right_side):
    return lax.dot_general(
        left_side, right_side, (((0,), (0,)), ((), ())), preferred_element_type=jnp.float32
    )


def block_parts(queries, key_rows, values, log_forget, doc_ids, prev_doc, block_len):
    length, head_count, feature = queries.shape
    block_count = length // block_len
    blocked = (block_count, block_len, head_count, feature)
    queries = queries.reshape(blocked)
    key_rows = key_rows.reshape(blocked)
    values = values.reshape(blocked)
    decays = jnp.cumsum(log_forget.reshape(blocked), axis=1)
    doc_ids = doc_ids.reshape(block_count, block_len)
    before = jnp.concatenate([jnp.reshape(prev_doc, (1,)), doc_ids[:-1, block_len - 1]])
    middle = decays[:, block_len // 2 : block_len // 2 + 1]
    final_decay = decays[:, block_len - 1 :]
    scores = jnp.einsum(
        "nthc,nshc->nhts",
        queries * jnp.exp(decays - middle),
        key_rows * jnp.exp(middle - decays),
        precision=HIGH,
    )
    causal = lax.broadcasted_iota(jnp.int32, (block_len, block_len), 0) >= lax.broadcasted_iota(
        jnp.int32, (block_len, block_len), 1
    )
    allowed = causal[None] & (doc_ids[:, :, None] == doc_ids[:, None, :])
    scores = jnp.where(allowed[:, None], scores, 0.0)
    inside = jnp.einsum("nhts,nshe->nthe", scores, values, precision=HIGH)
    in_tail = (doc_ids == doc_ids[:, block_len - 1 :]).astype(decays.dtype)
    ending = key_rows * jnp.exp(final_decay - decays) * in_tail[:, :, None, None]
    states = jnp.einsum("nshc,nshe->nhce", ending, values, precision=HIGH)
    kept_flag = (doc_ids[:, block_len - 1] == before).astype(decays.dtype)
    carried = jnp.exp(final_decay[:, 0]) * kept_flag[:, None, None]
    entering = (doc_ids == before[:, None]).astype(decays.dtype)
    reached = queries * jnp.exp(decays) * entering[:, :, None, None]
    prefix_decay, prefix_state = lax.associative_scan(chain_link, (carried, states), axis=0)
    return (inside, reached, prefix_decay, prefix_state)


def finish(pieces, state_in):
    inside, reached, prefix_decay, prefix_state = pieces
    state_ends = prefix_decay[..., None] * state_in[None] + prefix_state
    state_starts = jnp.concatenate([state_in[None], state_ends[:-1]], axis=0)
    outside = jnp.einsum("nthc,nhce->nthe", reached, state_starts, precision=HIGH)
    summed = inside + outside
    block_count, block_len, head_count, feature = summed.shape
    return (summed.reshape(block_count * block_len, head_count, feature), state_ends[-1])


def body(
    block_in,
    query_proj,
    forget_proj,
    value_proj,
    outgate_proj,
    out_proj,
    ffn_gate,
    ffn_up,
    ffn_down,
    first_gain,
    second_gain,
    group_gain,
    forget_bias,
    bound_table,
    layer_index,
    second_start,
    cotangent,
):
    row_count = block_in.shape[0]
    local_width = query_proj.shape[1]
    head_count = local_width // HEAD
    hidden_width = ffn_gate.shape[1]
    inputs = block_in.astype(jnp.float32)
    first_low = rms_norm(inputs, first_gain).astype(jnp.bfloat16)
    mix_local = jnp.concatenate([query_proj, forget_proj, value_proj, outgate_proj], axis=1)
    ffn_local = jnp.concatenate([ffn_gate, ffn_up], axis=1)
    mix_full, out_full = (
        lax.all_gather(mix_local, "dp", axis=0, tiled=True),
        lax.all_gather(out_proj, "dp", axis=1, tiled=True),
    )
    projected = jnp.dot(first_low, mix_full, preferred_element_type=jnp.float32)
    pre_query = projected[:, :local_width]
    pre_forget = projected[:, local_width : 2 * local_width]
    pre_value = projected[:, 2 * local_width : 3 * local_width]
    pre_outgate = projected[:, 3 * local_width :]
    bound_vec = lower_bound(bound_table, layer_index)
    queries, key_rows, log_forget = gate_values(pre_query, pre_forget, forget_bias, bound_vec)
    offset = lax.axis_index("ctx") * row_count
    doc_ids = (offset + lax.iota(jnp.int32, row_count) >= second_start[0]).astype(jnp.int32)
    prev_doc = (offset - 1 >= second_start[0]).astype(jnp.int32)

    def to_heads(flat):
        return flat.reshape(row_count, head_count, HEAD)

    def mixer(queries_in, keys_in, values_in, logs_in, state_in):
        return finish(
            block_parts(queries_in, keys_in, values_in, logs_in, doc_ids, prev_doc, BLOCK), state_in
        )

    pieces = block_parts(
        to_heads(queries),
        to_heads(key_rows),
        to_heads(pre_value),
        to_heads(log_forget),
        doc_ids,
        prev_doc,
        BLOCK,
    )
    identity = (
        jnp.ones((head_count, HEAD), jnp.float32),
        jnp.zeros((head_count, HEAD, HEAD), jnp.float32),
    )
    shard_decay = pieces[2][-1]
    entry_pair = carried_in((shard_decay, pieces[3][-1]), "ctx", chain_link, identity)
    state_in = entry_pair[1]
    mixed, _ = finish(pieces, state_in)
    mixed_flat = mixed.reshape(row_count, local_width)
    gated_low = head_norm(mixed_flat, pre_outgate, group_gain, head_count).astype(jnp.bfloat16)
    mix_partial = jnp.dot(gated_low, out_full, preferred_element_type=jnp.float32)
    resid = inputs + lax.psum(mix_partial, "tp")
    second_low = rms_norm(resid, second_gain).astype(jnp.bfloat16)
    ffn_full, down_full = (
        lax.all_gather(ffn_local, "dp", axis=0, tiled=True),
        lax.all_gather(ffn_down, "dp", axis=1, tiled=True),
    )
    gate_up = jnp.dot(second_low, ffn_full, preferred_element_type=jnp.float32)
    pre_gate = gate_up[:, :hidden_width]
    pre_up = gate_up[:, hidden_width:]
    hidden_low = (jax.nn.silu(pre_gate) * pre_up).astype(jnp.bfloat16)
    ffn_partial = jnp.dot(hidden_low, down_full, preferred_element_type=jnp.float32)
    block_out = (
        resid + lax.psum(ffn_partial.astype(jnp.bfloat16), "tp").astype(jnp.float32)
    ).astype(jnp.bfloat16)
    mix_full, out_full, ffn_full, down_full = (
        lax.all_gather(mix_local, "dp", axis=0, tiled=True),
        lax.all_gather(out_proj, "dp", axis=1, tiled=True),
        lax.all_gather(ffn_local, "dp", axis=0, tiled=True),
        lax.all_gather(ffn_down, "dp", axis=1, tiled=True),
    )
    cotangent_full = cotangent.astype(jnp.float32)
    hidden_grad = contract_last(cotangent, down_full)
    down_weight_grad = contract_first(hidden_low, cotangent)
    _, act_pull = jax.vjp(lambda gate_in, up_in: jax.nn.silu(gate_in) * up_in, pre_gate, pre_up)
    gate_grad, up_grad = act_pull(hidden_grad)
    gate_up_grad = jnp.concatenate([gate_grad, up_grad], axis=1).astype(jnp.bfloat16)
    second_part = contract_last(gate_up_grad, ffn_full)
    ffn_weight_grad = contract_first(second_low, gate_up_grad)
    second_total = lax.psum(second_part, "tp")
    _, second_pull = jax.vjp(rms_norm, resid, second_gain)
    resid_part, second_gain_grad = second_pull(second_total)
    resid_grad = cotangent_full + resid_part
    resid_low = resid_grad.astype(jnp.bfloat16)
    gated_grad = contract_last(resid_low, out_full)
    out_weight_grad = contract_first(gated_low, resid_low)
    _, head_pull = jax.vjp(
        lambda mixed_in, gate_in, gain_in: head_norm(mixed_in, gate_in, gain_in, head_count),
        mixed_flat,
        pre_outgate,
        group_gain,
    )
    mixed_grad, outgate_pre_grad, group_gain_grad = head_pull(gated_grad)
    _, mixer_pull = jax.vjp(
        mixer,
        to_heads(queries),
        to_heads(key_rows),
        to_heads(pre_value),
        to_heads(log_forget),
        state_in,
    )
    first_pass = mixer_pull(
        (to_heads(mixed_grad), jnp.zeros((head_count, HEAD, HEAD), jnp.float32))
    )
    after_pair = carried_in_2((shard_decay, first_pass[4]), "ctx", chain_link, identity)
    second_pass = mixer_pull((jnp.zeros((row_count, head_count, HEAD), jnp.float32), after_pair[1]))
    query_rec_grad = (first_pass[0] + second_pass[0]).reshape(row_count, local_width)
    key_rec_grad = (first_pass[1] + second_pass[1]).reshape(row_count, local_width)
    value_rec_grad = (first_pass[2] + second_pass[2]).reshape(row_count, local_width)
    log_rec_grad = (first_pass[3] + second_pass[3]).reshape(row_count, local_width)
    _, gate_pull = jax.vjp(gate_values, pre_query, pre_forget, forget_bias, bound_vec)
    query_pre_grad, forget_pre_grad, forget_bias_grad, bound_grad = gate_pull(
        (query_rec_grad, key_rec_grad, log_rec_grad)
    )
    _, table_pull = jax.vjp(lambda rows_in: lower_bound(rows_in, layer_index), bound_table)
    (table_grad,) = table_pull(bound_grad)
    proj_grad = jnp.concatenate(
        [query_pre_grad, forget_pre_grad, value_rec_grad, outgate_pre_grad], axis=1
    ).astype(jnp.bfloat16)
    first_part = contract_last(proj_grad, mix_full)
    mix_weight_grad = contract_first(first_low, proj_grad)
    first_total = lax.psum(first_part.astype(jnp.bfloat16), "tp").astype(jnp.float32)
    _, first_pull = jax.vjp(rms_norm, inputs, first_gain)
    input_part, first_gain_grad = first_pull(first_total)
    input_grad = resid_grad + input_part
    mix_summed, out_summed, ffn_summed, down_summed = (
        lax.psum_scatter(
            mix_weight_grad.astype(jnp.bfloat16), ("dp", "ctx"), scatter_dimension=0, tiled=True
        ).astype(jnp.float32),
        lax.psum_scatter(
            out_weight_grad.astype(jnp.bfloat16), ("dp", "ctx"), scatter_dimension=1, tiled=True
        ).astype(jnp.float32),
        lax.psum_scatter(
            ffn_weight_grad.astype(jnp.bfloat16), ("dp", "ctx"), scatter_dimension=0, tiled=True
        ).astype(jnp.float32),
        lax.psum_scatter(
            down_weight_grad.astype(jnp.bfloat16), ("dp", "ctx"), scatter_dimension=1, tiled=True
        ).astype(jnp.float32),
    )
    mix_shard, out_shard, ffn_shard, down_shard = (
        lax.all_gather(mix_summed.astype(jnp.bfloat16), "ctx", axis=0, tiled=True).astype(
            mix_summed.dtype
        ),
        lax.all_gather(out_summed.astype(jnp.bfloat16), "ctx", axis=1, tiled=True).astype(
            out_summed.dtype
        ),
        lax.all_gather(ffn_summed.astype(jnp.bfloat16), "ctx", axis=0, tiled=True).astype(
            ffn_summed.dtype
        ),
        lax.all_gather(down_summed.astype(jnp.bfloat16), "ctx", axis=1, tiled=True).astype(
            down_summed.dtype
        ),
    )
    first_sum, second_sum, group_sum, bias_sum, table_sum = (
        lax.psum(first_gain_grad.astype(jnp.bfloat16), ("dp", "ctx")).astype(jnp.float32),
        lax.psum(second_gain_grad.astype(jnp.bfloat16), ("dp", "ctx")).astype(jnp.float32),
        lax.psum(group_gain_grad.astype(jnp.bfloat16), ("dp", "ctx")).astype(jnp.float32),
        lax.psum(forget_bias_grad.astype(jnp.bfloat16), ("dp", "ctx")).astype(jnp.float32),
        lax.psum(table_grad.astype(jnp.bfloat16), ("dp", "ctx")).astype(jnp.float32),
    )
    return (
        block_out,
        input_grad,
        mix_shard[:, :local_width],
        mix_shard[:, local_width : 2 * local_width],
        mix_shard[:, 2 * local_width : 3 * local_width],
        mix_shard[:, 3 * local_width :],
        out_shard,
        ffn_shard[:, :hidden_width],
        ffn_shard[:, hidden_width:],
        down_shard,
        first_sum,
        second_sum,
        group_sum,
        bias_sum,
        table_sum,
    )


def solution(mesh):
    return jax.shard_map(
        body,
        mesh=mesh,
        in_specs=(
            P(("dp", "ctx"), None),
            P("dp", "tp"),
            P("dp", "tp"),
            P("dp", "tp"),
            P("dp", "tp"),
            P("tp", "dp"),
            P("dp", "tp"),
            P("dp", "tp"),
            P("tp", "dp"),
            P(),
            P(),
            P("tp"),
            P("tp"),
            P(None, "tp"),
            P(),
            P("dp"),
            P(("dp", "ctx"), None),
        ),
        out_specs=(
            P(("dp", "ctx"), None),
            P(("dp", "ctx"), None),
            P("dp", "tp"),
            P("dp", "tp"),
            P("dp", "tp"),
            P("dp", "tp"),
            P("tp", "dp"),
            P("dp", "tp"),
            P("dp", "tp"),
            P("tp", "dp"),
            P(),
            P(),
            P("tp"),
            P("tp"),
            P(None, "tp"),
        ),
        check_vma=False,
    )
```

profile of v0, /device:TPU:0, one launch (start us, length us, event | category | flops | bytes accessed | tf_op | source)
XLA Modules:
  0.0 2218.8 jit_solution(17821822070272523341)
XLA Ops:
  17.0 145.9 %all-gather.8.cloned.1.call-done = bf16[2048,2048]{1,0:T(8,128)(2,1)} async-done(((bf16[512,2048]{1,0:T(8,128)(2,1)}), bf16[2048,2048]{1,0:T(8,128)(2,1)}) %all-gather.8.cloned.1.call-update) | async-done | bytes 8388624 | tf_op jit(solution)/shard_map/all_gather | solution.py:170
  162.8 12.6 fusion.115
  199.7 6.4 fusion.105
  209.9 13.7 fusion.85
  248.3 7.0 pad.555
  268.4 18.6 pad.557
  287.0 12.1 pad.558
  299.2 6.7 add.591
  312.1 35.5 %pad.734 = f32[31,4,128,128]{2,3,1,0:T(8,128)} pad(f32[16,4,128,128]{2,3,1,0:T(8,128)} %pad_maximum_fusion.5, f32[]{:T(128)} %constant.113.clone.1), padding=0_0_1x0_0_0x0_0_0x0_0_0 | pad | bytes 12320772 | tf_op jit(solution)/shard_map/slice | solution.py:135
  347.6 35.6 %pad.559 = f32[32,4,128,128]{2,3,1,0:T(8,128)} pad(f32[16,4,128,128]{2,3,1,0:T(8,128)} %pad_maximum_fusion.5, f32[]{:T(128)} %constant.113.clone.1), padding=0_1_1x0_0_0x0_0_0x0_0_0 | pad | bytes 12582916 | tf_op jit(solution)/shard_map/pad | solution.py:128
  385.0 35.6 %pad.1005 = f32[32,4,128,128]{2,3,1,0:T(8,128)} pad(f32[16,4,128,128]{2,3,1,0:T(8,128)} %add.591, f32[]{:T(128)} %constant.113.clone.1), padding=1_0_1x0_0_0x0_0_0x0_0_0 | pad | bytes 12582916
  438.1 12.0 multiply_add_fusion
  450.2 16.1 fusion.19
  487.9 7.6 fusion.207
  499.8 166.2 %all-reduce.122.cloned.1.call-done = f32[1024,2048]{1,0:T(8,128)} async-done(((f32[1024,2048]{1,0:T(8,128)}), f32[1024,2048]{1,0:T(8,128)}) %all-reduce.122.cloned.1.call-update) | async-done | bytes 8388624 | tf_op jit(solution)/shard_map/psum | solution.py:212
  666.0 9.0 multiply_reduce_fusion.4
  675.0 194.9 %all-gather.12.cloned.1.call-done = bf16[2048,2816]{1,0:T(8,128)(2,1)} async-done(((bf16[512,2816]{1,0:T(8,128)(2,1)}), bf16[2048,2816]{1,0:T(8,128)(2,1)}) %all-gather.12.cloned.1.call-update) | async-done | bytes 11534352 | tf_op jit(solution)/shard_map/all_gather | solution.py:215
  869.9 20.0 fusion.177
  889.9 86.4 %all-gather.14.cloned.1.call-done = bf16[1408,2048]{1,0:T(8,128)(2,1)} async-done(((bf16[1408,512]{1,0:T(8,128)(2,1)}), bf16[1408,2048]{1,0:T(8,128)(2,1)}) %all-gather.14.cloned.1.call-update) | async-done | bytes 5767184 | tf_op jit(solution)/shard_map/all_gather | solution.py:216
  976.3 16.2 fusion.15
  995.1 16.8 fusion.20
  1012.0 10.5 convolution_convert_fusion.1
  1024.9 11.3 fusion.17
  1045.9 8.9 fusion.76
  1054.8 18.7 convolution_convert_fusion
  1073.5 11.1 convolution_convert_fusion.4
  1084.6 97.8 %all-reduce.124.cloned.1.call-done = f32[1024,2048]{1,0:T(8,128)} async-done(((f32[1024,2048]{1,0:T(8,128)}), f32[1024,2048]{1,0:T(8,128)}) %all-reduce.124.cloned.1.call-update) | async-done | bytes 8388624 | tf_op jit(solution)/shard_map/psum | solution.py:240
  1182.4 7.7 multiply_reduce_fusion
  1197.1 7.8 broadcast_multiply_fusion.4
  1214.6 13.5 fusion.78
  1241.9 9.7 fusion.12
  1256.5 9.1 multiply_reduce_fusion.7
  1364.9 10.2 pad.622
  1391.8 8.7 multiply_reduce_fusion.11
  1401.0 12.0 pad.589
  1413.1 18.5 pad.623
  1435.8 18.6 pad.624
  1454.4 12.1 pad.590
  1466.5 16.7 pad.568
  1483.2 10.8 pad.602
  1494.0 15.5 multiply_reduce_fusion.5
  1510.5 35.6 %pad.625 = f32[32,4,128,128]{2,3,1,0:T(8,128)} pad(f32[16,4,128,128]{2,3,1,0:T(8,128)} %get-tuple-element.256, f32[]{:T(128)} %constant.113.clone.1), padding=1_0_1x0_0_0x0_0_0x0_0_0 | pad | bytes 12582916 | tf_op jit(solution)/shard_map/transpose(jvp())/pad | solution.py:128
  1546.0 35.5 %pad.591 = f32[32,4,128,128]{2,3,1,0:T(8,128)} pad(f32[16,4,128,128]{2,3,1,0:T(8,128)} %get-tuple-element.255, f32[]{:T(128)} %constant.113.clone.1), padding=1_0_1x0_0_0x0_0_0x0_0_0 | pad | bytes 12582916 | tf_op jit(solution)/shard_map/transpose(jvp())/pad | solution.py:128
  1581.5 8.8 broadcast_multiply_fusion.1
  1590.3 35.6 %pad.592 = f32[32,4,128,128]{2,3,1,0:T(8,128)} pad(f32[16,4,128,128]{2,3,1,0:T(8,128)} %get-tuple-element.375, f32[]{:T(128)} %constant.113.clone.1), padding=0_1_1x0_0_0x0_0_0x0_0_0 | pad | bytes 12582916 | tf_op jit(solution)/shard_map/transpose(jvp())/pad | solution.py:128
  1625.9 35.7 %pad.626 = f32[32,4,128,128]{2,3,1,0:T(8,128)} pad(f32[16,4,128,128]{2,3,1,0:T(8,128)} %get-tuple-element.376, f32[]{:T(128)} %constant.113.clone.1), padding=0_1_1x0_0_0x0_0_0x0_0_0 | pad | bytes 12582916 | tf_op jit(solution)/shard_map/transpose(jvp())/pad | solution.py:128
  1661.7 33.6 %pad.562 = f32[32,4,128,128]{2,3,1,0:T(8,128)} pad(f32[15,4,128,128]{2,3,1,0:T(8,128)} %get-tuple-element.290, f32[]{:T(128)} %constant.113.clone.1), padding=2_1_1x0_0_0x0_0_0x0_0_0 | pad | bytes 12320772 | tf_op jit(solution)/shard_map/transpose(jvp())/pad | solution.py:128
  1695.3 33.7 %pad.597 = f32[32,4,128,128]{2,3,1,0:T(8,128)} pad(f32[15,4,128,128]{2,3,1,0:T(8,128)} %get-tuple-element.291, f32[]{:T(128)} %constant.113.clone.1), padding=2_1_1x0_0_0x0_0_0x0_0_0 | pad | bytes 12320772 | tf_op jit(solution)/shard_map/transpose(jvp())/pad | solution.py:128
  1729.0 10.8 fusion.18
  1752.8 10.0 add_add_fusion.3
  1762.8 8.6 fusion.103
  1771.4 15.1 fusion.83
  1786.5 9.8 add_add_fusion.2
  1796.3 8.6 fusion.101
  1810.3 19.3 fusion.176
  1830.9 11.6 fusion.41
  1842.6 13.5 fusion.81
  1877.1 12.9 convolution_convert_fusion.3
  1890.7 14.5 convolution_convert_fusion.2
  1913.4 152.0 %all-reduce.126.cloned.1.call-done = (bf16[1024,2048]{1,0:T(8,128)(2,1)}, bf16[1024,2048]{1,0:T(8,128)(2,1)}) async-done(((bf16[1024,2048]{1,0:T(8,128)(2,1)}, bf16[1024,2048]{1,0:T(8,128)(2,1)}), (bf16[1024,2048]{1,0:T(8,128)(2,1)}, bf16[1024,2048]{1,0:T(8,128)(2,1)})) %all-reduce.126.cloned.1.call-update) | async-done | bytes 8388624 | tf_op jit(solution)/shard_map/psum | solution.py:224
  2065.4 8.4 add_convert_fusion
  2073.8 84.8 %reduce-scatter.5.cloned.1.call-done = bf16[256,2048]{1,0:T(8,128)(2,1)} async-done(((bf16[2048,2048]{1,0:T(8,128)(2,1)}), bf16[256,2048]{1,0:T(8,128)(2,1)}) %reduce-scatter.5.cloned.1.call-update) | async-done | bytes 1048592 | tf_op jit(solution)/shard_map/reduce_scatter | solution.py:287
  2164.6 26.3 %all-reduce.116 = (bf16[2048]{0:T(1024)(128)(2,1)S(1)}, bf16[2048]{0:T(1024)(128)(2,1)S(1)}, bf16[512]{0:T(512)(128)(2,1)S(1)}, bf16[512]{0:T(512)(128)(2,1)S(1)}, bf16[24,512]{1,0:T(8,128)(2,1)S(1)}) all-reduce(bf16[2048]{0:T(1024)(128)(2,1)S(1)} %get-tuple-element.200, ...), channel_id=1, replica_groups=mesh['dp'=4,'ctx'=2,'tp'=4] {'dp','ctx'}, use_global_device_ids=true, to_apply=%region_51.52 | all-reduce | flops 17408 | bytes 69632 | tf_op jit(solution)/shard_map/psum | solution.py:315
  2193.9 9.5 fusion.6
  (792 shorter events, 362.1 us)
Async XLA Ops:
  7.2 155.7 %all-gather.8.cloned.1.call-start = ((), (), s32[]{:S(2)}) async-start(), calls=%async_computation.4 | async-start | bytes 10485760 | tf_op jit(solution)/shard_map/all_gather | solution.py:170
  10.4 477.5 %all-gather.10.cloned.1.call-start = ((), (), s32[]{:S(2)}) async-start(), calls=%async_computation.5 | async-start | bytes 2621440 | tf_op jit(solution)/shard_map/all_gather | solution.py:171
  11.1 654.9 %all-reduce.122.cloned.1.call-start = ((), (), s32[]{:S(2)}) async-start(), calls=%async_computation.6 | async-start | bytes 16777216 | tf_op jit(solution)/shard_map/psum | solution.py:212
  12.7 150.1 %copy-start.194 = (f32[2048]{0:T(1024)S(1)}, f32[2048]{0:T(1024)}, u32[]{:S(2)}) copy-start(f32[2048]{0:T(1024)} %param.28) | copy-start | bytes 24580
  16.4 159.0 %copy-start.171 = (f32[1024]{0:T(1024)}, f32[1024]{0:T(1024)S(1)}, u32[]{:S(2)}) copy-start(f32[1024]{0:T(1024)S(1)} %fusion.149) | copy-start | bytes 12292
  16.6 158.8 %copy-start.178 = (f32[512]{0:T(512)}, f32[512]{0:T(512)S(1)}, u32[]{:S(2)}) copy-start(f32[512]{0:T(512)S(1)} %multiply_reduce_fusion.28) | copy-start | bytes 6148
  16.6 158.8 %copy-start.196 = (f32[512]{0:T(512)}, f32[512]{0:T(512)S(1)}, u32[]{:S(2)}) copy-start(f32[512]{0:T(512)S(1)} %broadcast_subtract_fusion) | copy-start | bytes 6148
  16.7 169.4 %copy-start.214 = (f32[32]{0:T(128)}, f32[32]{0:T(128)S(1)}, u32[]{:S(2)}) copy-start(f32[32]{0:T(128)S(1)} %get-tuple-element.269) | copy-start | bytes 388
  16.9 1024.1 %copy-start.73 = (pred[32,32,32]{2,1,0:T(8,128)(4,1)}, pred[32,32,32]{2,1,0:T(8,128)(4,1)S(1)}, u32[]{:S(2)}) copy-start(pred[32,32,32]{2,1,0:T(8,128)(4,1)S(1)} %compare_and_fusion) | copy-start | bytes 98308
  16.9 189.3 %copy-start.131 = (f32[32,32]{0,1:T(8,128)}, f32[32,32]{0,1:T(8,128)S(1)}, u32[]{:S(2)}) copy-start(f32[32,32]{0,1:T(8,128)S(1)} %get-tuple-element.440) | copy-start | bytes 12292
  16.9 415.8 %copy-start.129 = (f32[32,32]{0,1:T(8,128)}, f32[32,32]{0,1:T(8,128)S(1)}, u32[]{:S(2)}) copy-start(f32[32,32]{0,1:T(8,128)S(1)} %get-tuple-element.439) | copy-start | bytes 12292
  17.0 158.5 %copy-start.204 = (f32[512]{0:T(512)S(1)}, f32[512]{0:T(512)}, u32[]{:S(2)}) copy-start(f32[512]{0:T(512)} %param.31) | copy-start | bytes 6148
  184.2 22.0 copy-start
  186.0 20.1 copy-start.109
  187.5 36.2 %copy-start.125 = (f32[16,4,128]{2,1,0:T(4,128)}, f32[16,4,128]{2,1,0:T(4,128)S(1)}, u32[]{:S(2)}) copy-start(f32[16,4,128]{2,1,0:T(4,128)S(1)} %get-tuple-element.356) | copy-start | bytes 98308
  187.5 39.7 %copy-start.142 = (f32[8,4,128]{2,1,0:T(4,128)}, f32[8,4,128]{2,1,0:T(4,128)S(1)}, u32[]{:S(2)}) copy-start(f32[8,4,128]{2,1,0:T(4,128)S(1)} %get-tuple-element.380) | copy-start | bytes 49156
  187.6 42.5 %copy-start.155 = (f32[4,4,128]{2,1,0:T(4,128)}, f32[4,4,128]{2,1,0:T(4,128)S(1)}, u32[]{:S(2)}) copy-start(f32[4,4,128]{2,1,0:T(4,128)S(1)} %get-tuple-element.402) | copy-start | bytes 24580
  187.6 42.6 %copy-start.165 = (f32[2,4,128]{2,1,0:T(4,128)}, f32[2,4,128]{2,1,0:T(4,128)S(1)}, u32[]{:S(2)}) copy-start(f32[2,4,128]{2,1,0:T(4,128)S(1)} %get-tuple-element.421) | copy-start | bytes 12292
  187.7 42.6 %copy-start.198 = (f32[4,128]{1,0:T(4,128)}, f32[4,128]{1,0:T(4,128)S(1)}, u32[]{:S(2)}) copy-start(f32[4,128]{1,0:T(4,128)S(1)} %get-tuple-element.431) | copy-start | bytes 6148
  229.3 17.0 copy-start.60
  268.4 18.6 copy-start.75
  347.6 35.6 %copy-start.206 = (f32[1,4,128]{2,1,0:T(4,128)S(1)}, f32[1,4,128]{2,1,0:T(4,128)}, u32[]{:S(2)}) copy-start(f32[1,4,128]{2,1,0:T(4,128)} %get-tuple-element.266) | copy-start | bytes 6148
  424.2 600.7 %copy-start.88 = (f32[1,4,128,128]{2,3,1,0:T(8,128)}, f32[1,4,128,128]{2,3,1,0:T(8,128)S(1)}, u32[]{:S(2)}) copy-start(f32[1,4,128,128]{2,3,1,0:T(8,128)S(1)} %add_select_fusion) | copy-start | bytes 786436
  450.2 16.1 copy-start.52
  450.2 16.1 copy-start.105
  495.5 374.3 %all-gather.12.cloned.1.call-start = ((), (), s32[]{:S(2)}) async-start(), calls=%async_computation.7 | async-start | bytes 14417920 | tf_op jit(solution)/shard_map/all_gather | solution.py:215
  499.2 477.1 %all-gather.14.cloned.1.call-start = ((), (), s32[]{:S(2)}) async-start(), calls=%async_computation.8 | async-start | bytes 7208960 | tf_op jit(solution)/shard_map/all_gather | solution.py:216
  499.7 370.1 %copy-start.177 = (f32[2048]{0:T(1024)S(1)}, f32[2048]{0:T(1024)}, u32[]{:S(2)}) copy-start(f32[2048]{0:T(1024)} %param.29) | copy-start | bytes 24580
  499.8 682.7 %all-reduce.124.cloned.1.call-start = ((), (), s32[]{:S(2)}) async-start(), calls=%async_computation.9 | async-start | bytes 16777216 | tf_op jit(solution)/shard_map/psum | solution.py:240
  1011.9 865.1 %reduce-scatter.11.cloned.1.call-start = ((), (), s32[]{:S(2)}) async-start(), calls=%async_computation.15 | async-start | bytes 6488064 | tf_op jit(solution)/shard_map/reduce_scatter | solution.py:296
  1022.5 882.9 %reduce-scatter.9.cloned.1.call-start = ((), (), s32[]{:S(2)}) async-start(), calls=%async_computation.13 | async-start | bytes 12976128 | tf_op jit(solution)/shard_map/reduce_scatter | solution.py:293
  1024.9 16.1 copy-start.59
  1073.5 833.1 %reduce-scatter.7.cloned.1.call-start = ((), (), s32[]{:S(2)}) async-start(), calls=%async_computation.12 | async-start | bytes 2359296 | tf_op jit(solution)/shard_map/reduce_scatter | solution.py:290
  1265.8 31.7 %copy-start.157 = (f32[8,4,128]{2,1,0:T(4,128)}, f32[8,4,128]{2,1,0:T(4,128)S(1)}, u32[]{:S(2)}) copy-start(f32[8,4,128]{2,1,0:T(4,128)S(1)} %slice.479) | copy-start | bytes 49156
  1265.9 31.7 %copy-start.158 = (f32[8,4,128]{2,1,0:T(4,128)}, f32[8,4,128]{2,1,0:T(4,128)S(1)}, u32[]{:S(2)}) copy-start(f32[8,4,128]{2,1,0:T(4,128)S(1)} %slice.471) | copy-start | bytes 49156
  1413.1 18.5 copy-start.143
  1435.8 18.6 copy-start.79
  1466.5 16.7 copy-start.82
  1494.0 15.5 slice-start.20
  1546.0 35.5 %copy-start.126 = (f32[16,4,128]{2,1,0:T(4,128)S(1)}, f32[16,4,128]{2,1,0:T(4,128)}, u32[]{:S(2)}) copy-start(f32[16,4,128]{2,1,0:T(4,128)} %copy-done.125) | copy-start | bytes 98308
  1695.3 33.7 %copy-start.24 = (f32[32,4,128,32]{2,3,1,0:T(8,128)S(1)}, f32[32,4,128,32]{2,3,1,0:T(8,128)}, u32[]{:S(2)}) copy-start(f32[32,4,128,32]{2,3,1,0:T(8,128)} %copy-done.23) | copy-start | bytes 6291460
  1695.3 33.7 %copy-start.89 = (f32[1,4,128,128]{2,3,1,0:T(8,128)S(1)}, f32[1,4,128,128]{2,3,1,0:T(8,128)}, u32[]{:S(2)}) copy-start(f32[1,4,128,128]{2,3,1,0:T(8,128)} %copy-done.88) | copy-start | bytes 786436
  1771.4 33.5 %slice-start.1 = ((s8[8388608]{0:T(1024)(128)(4,1)}), s8[4194304]{0:T(1024)(128)(4,1)S(1)}, s32[]{:S(2)}) async-start(s8[8388608]{0:T(1024)(128)(4,1)} %bitcast.242), calls=%async_computation.19 | async-start | bytes 8388608
  1786.5 18.4 slice-start.2
  1808.7 20.9 copy-start.134
  1808.7 20.9 copy-start.135
  1808.7 20.9 slice-start.17
  1808.7 20.9 slice-start.18
  1808.8 20.9 copy-start.215
  1808.8 101.3 %all-gather.20.cloned.1.call-start = ((), (), s32[]{:S(2)}) async-start(), calls=%async_computation.16 | async-start | bytes 2162688 | tf_op jit(solution)/shard_map/all_gather | solution.py:310
  1810.3 20.6 copy-start.7
  1810.3 20.6 copy-start.11
  1810.3 20.6 copy-start.30
  1810.3 20.6 copy-start.47
  1810.3 20.6 copy-start.48
  1810.3 20.6 copy-start.49
  1810.3 20.6 copy-start.54
  1810.3 20.6 copy-start.55
  1810.3 20.6 copy-start.78
  1877.1 188.4 %all-reduce.126.cloned.1.call-start = ((), (), s32[]{:S(2)}) async-start(), calls=%async_computation.17 | async-start | bytes 16777216 | tf_op jit(solution)/shard_map/psum | solution.py:224
  1890.0 268.6 %reduce-scatter.5.cloned.1.call-start = ((), (), s32[]{:S(2)}) async-start(), calls=%async_computation.10 | async-start | bytes 9437184 | tf_op jit(solution)/shard_map/reduce_scatter | solution.py:287
  1905.3 298.1 %all-gather.18.cloned.1.call-start = ((), (), s32[]{:S(2)}) async-start(), calls=%async_computation.14 | async-start | bytes 4325376 | tf_op jit(solution)/shard_map/all_gather | solution.py:307
  1906.0 302.0 %all-gather.16.cloned.1.call-start = ((), (), s32[]{:S(2)}) async-start(), calls=%async_computation.11 | async-start | bytes 3145728 | tf_op jit(solution)/shard_map/all_gather | solution.py:301
  2158.6 35.2 %copy-start.168 = (f32[1024]{0:T(1024)S(1)}, f32[1024]{0:T(1024)}, u32[]{:S(2)}) copy-start(f32[1024]{0:T(1024)} %copy-done.167) | copy-start | bytes 12292
  (197 other events, 961.7 us)
Sparse Core Ops, SparseCore 0:
  10.5 152.3 all-gather.7
  164.4 44.1 all-gather.9
  495.6 170.3 all-reduce.121
  668.1 201.7 all-gather.11
  871.3 104.8 all-gather.13
  1012.0 170.3 all-reduce.123
  1184.7 65.5 reduce-scatter.10
  1252.6 117.6 reduce-scatter.8
  1808.8 36.2 reduce-scatter.6
  1877.2 10.0 all-gather.19
  1891.6 173.7 all-reduce.125
  2068.3 90.2 reduce-scatter.4
  2160.2 10.1 all-gather.17
  2171.8 11.7 all-gather.15
where the time goes:
time: 2250 us; the launch traced here: 2220 us
  waiting for transfers between devices  930 us (41%)
  local copies, waits for them, and re-layouts  640 us (28%)
  matrix products  319 us (14%)
  other arithmetic  275 us (12%)
  blocking collectives  36.4 us (2%)
    pad x74, local copies, waits for them, and re-layouts, block_parts(): lax.associative_scan(chain_link, (carried, states), axis=0)  483 us
    all_gather x1, waiting for transfers between devices, body(): lax.all_gather(ffn_local, 'dp', axis=0, tiled=True)  195 us
    psum x1, waiting for transfers between devices, body(): resid = inputs + lax.psum(mix_partial, 'tp')  166 us
    psum x1, waiting for transfers between devices, body(): lax.psum(ffn_partial.astype(jnp.bfloat16), 'tp').astype(jnp.float32)  152 us
    all_gather x1, waiting for transfers between devices, body(): lax.all_gather(mix_local, 'dp', axis=0, tiled=True)  146 us
    psum x1, waiting for transfers between devices, body(): second_total = lax.psum(second_part, 'tp')  97.8 us
    all_gather x1, waiting for transfers between devices, body(): lax.all_gather(ffn_down, 'dp', axis=1, tiled=True)  86.4 us
    reduce_scatter x1, waiting for transfers between devices, body(): lax.psum_scatter(mix_weight_grad.astype(jnp.bfloat16), ('dp', 'ctx'), sca...  84.8 us
  transfers between devices with their start and end apart: 14, of which 7 were waited for; matrix products, arithmetic and copies ran while one was open for 51% of the time, Pallas kernels for 0%

commit v1 on v0

--- a/solution.py
+++ b/solution.py
@@ -8,6 +8,15 @@
 HIGH = lax.Precision.HIGHEST
 EPS_NORM = 1e-06
 EPS_GROUP = 1e-05
+
+
+def doubling_sum(x, mesh_axis):
+    n_dev = lax.axis_size(mesh_axis)
+    acc, far = (x, 1)
+    while far < n_dev:
+        acc = acc + lax.ppermute(acc, mesh_axis, [(i, i ^ far) for i in range(n_dev)])
+        far = 2 * far
+    return acc
 
 
 def carried_in(value, axis, join, neutral):
@@ -237,7 +246,7 @@
     gate_up_grad = jnp.concatenate([gate_grad, up_grad], axis=1).astype(jnp.bfloat16)
     second_part = contract_last(gate_up_grad, ffn_full)
     ffn_weight_grad = contract_first(second_low, gate_up_grad)
-    second_total = lax.psum(second_part, "tp")
+    second_total = doubling_sum(second_part, "tp")
     _, second_pull = jax.vjp(rms_norm, resid, second_gain)
     resid_part, second_gain_grad = second_pull(second_total)
     resid_grad = cotangent_full + resid_part

time: 2250 us -> 2470 us (1.098)
  waiting for transfers between devices: 930 us -> 1150 us
  local copies, waits for them, and re-layouts: 640 us -> 602 us
    ppermute x0 -> x2, waiting for transfers between devices: none -> 322 us  [doubling_sum(): lax.ppermute(acc, mesh_axis, [(i, i ^ far) for i in range(n_dev)])]
    psum x1 -> x0, waiting for transfers between devices: 97.8 us -> none  [body(): second_total = lax.psum(second_part, 'tp')]
    pad x74, local copies, waits for them, and re-layouts: 483 us -> 456 us  [block_parts(): lax.associative_scan(chain_link, (carried, states), axis=0)]
    unnamed x468 -> x426, local copies, waits for them, and re-layouts: 79.2 us -> 67.2 us
  transfers between devices with their start and end apart: 14 -> 15, of which waited for: 7 -> 8; matrix products, arithmetic and copies ran while one was open for 51% -> 47% of each run, Pallas kernels for 0% -> 0%
where the time goes in v1:
time: 2470 us; the launch traced here: 2430 us
  waiting for transfers between devices  1150 us (47%)
  local copies, waits for them, and re-layouts  602 us (24%)
  matrix products  323 us (13%)
  other arithmetic  297 us (12%)
  blocking collectives  36.4 us (1%)
    pad x74, local copies, waits for them, and re-layouts, block_parts(): lax.associative_scan(chain_link, (carried, states), axis=0)  456 us
    ppermute x2, waiting for transfers between devices, doubling_sum(): lax.ppermute(acc, mesh_axis, [(i, i ^ far) for i in range(n_dev)])  322 us
    all_gather x1, waiting for transfers between devices, body(): lax.all_gather(ffn_local, 'dp', axis=0, tiled=True)  195 us
    psum x1, waiting for transfers between devices, body(): resid = inputs + lax.psum(mix_partial, 'tp')  166 us
    psum x1, waiting for transfers between devices, body(): lax.psum(ffn_partial.astype(jnp.bfloat16), 'tp').astype(jnp.float32)  148 us
    all_gather x1, waiting for transfers between devices, body(): lax.all_gather(mix_local, 'dp', axis=0, tiled=True)  146 us
    all_gather x1, waiting for transfers between devices, body(): lax.all_gather(ffn_down, 'dp', axis=1, tiled=True)  86.4 us
    reduce_scatter x1, waiting for transfers between devices, body(): lax.psum_scatter(mix_weight_grad.astype(jnp.bfloat16), ('dp', 'ctx'), sca...  84.9 us
  transfers between devices with their start and end apart: 15, of which 8 were waited for; matrix products, arithmetic and copies ran while one was open for 47% of the time, Pallas kernels for 0%

profile of v1, /device:TPU:0, one launch (start us, length us, event | category | flops | bytes accessed | tf_op | source)
XLA Modules:
  0.0 2430.6 jit_solution(1689016389080359105)
XLA Ops:
  17.0 145.9 %all-gather.8.cloned.1.call-done = bf16[2048,2048]{1,0:T(8,128)(2,1)} async-done(((bf16[512,2048]{1,0:T(8,128)(2,1)}), bf16[2048,2048]{1,0:T(8,128)(2,1)}) %all-gather.8.cloned.1.call-update) | async-done | bytes 8388624 | tf_op jit(solution)/shard_map/all_gather | solution.py:179
  162.8 12.6 fusion.115
  209.9 13.5 fusion.85
  268.2 18.6 pad.557
  286.8 12.1 pad.558
  311.9 35.5 %pad.734 = f32[31,4,128,128]{2,3,1,0:T(8,128)} pad(f32[16,4,128,128]{2,3,1,0:T(8,128)} %pad_maximum_fusion.5, f32[]{:T(128)} %constant.113.clone.1), padding=0_0_1x0_0_0x0_0_0x0_0_0 | pad | bytes 12320772 | tf_op jit(solution)/shard_map/slice | solution.py:144
  347.5 35.8 %pad.559 = f32[32,4,128,128]{2,3,1,0:T(8,128)} pad(f32[16,4,128,128]{2,3,1,0:T(8,128)} %pad_maximum_fusion.5, f32[]{:T(128)} %constant.113.clone.1), padding=0_1_1x0_0_0x0_0_0x0_0_0 | pad | bytes 12582916 | tf_op jit(solution)/shard_map/pad | solution.py:137
  385.0 35.8 %pad.1005 = f32[32,4,128,128]{2,3,1,0:T(8,128)} pad(f32[16,4,128,128]{2,3,1,0:T(8,128)} %add.595, f32[]{:T(128)} %constant.113.clone.1), padding=1_0_1x0_0_0x0_0_0x0_0_0 | pad | bytes 12582916
  438.5 11.7 multiply_add_fusion
  450.2 15.9 fusion.19
  487.9 7.5 fusion.207
  499.8 166.2 %all-reduce.121.cloned.1.call-done = f32[1024,2048]{1,0:T(8,128)} async-done(((f32[1024,2048]{1,0:T(8,128)}), f32[1024,2048]{1,0:T(8,128)}) %all-reduce.121.cloned.1.call-update) | async-done | bytes 8388624 | tf_op jit(solution)/shard_map/psum | solution.py:221
  665.9 9.0 multiply_reduce_fusion.4
  674.9 194.9 %all-gather.12.cloned.1.call-done = bf16[2048,2816]{1,0:T(8,128)(2,1)} async-done(((bf16[512,2816]{1,0:T(8,128)(2,1)}), bf16[2048,2816]{1,0:T(8,128)(2,1)}) %all-gather.12.cloned.1.call-update) | async-done | bytes 11534352 | tf_op jit(solution)/shard_map/all_gather | solution.py:224
  869.8 20.1 fusion.177
  889.9 86.4 %all-gather.14.cloned.1.call-done = bf16[1408,2048]{1,0:T(8,128)(2,1)} async-done(((bf16[1408,512]{1,0:T(8,128)(2,1)}), bf16[1408,2048]{1,0:T(8,128)(2,1)}) %all-gather.14.cloned.1.call-update) | async-done | bytes 5767184 | tf_op jit(solution)/shard_map/all_gather | solution.py:225
  976.2 16.9 fusion.15
  994.7 8.1 convolution_convert_fusion.1
  1002.9 19.4 convolution_convert_fusion
  1022.3 18.9 fusion.20
  1042.7 181.3 %collective-permute-done = f32[1024,2048]{1,0:T(8,128)} collective-permute-done((f32[1024,2048]{1,0:T(8,128)}, f32[1024,2048]{1,0:T(8,128)}, u32[]{:S(2)}, u32[]{:S(2)}) %collective-permute-start) | collective-permute-done | bytes 8388640 | tf_op jit(solution)/shard_map/ppermute | solution.py:17
  1223.9 11.7 add.608
  1238.9 10.9 fusion.17
  1259.6 8.9 fusion.76
  1268.5 8.2 convolution_convert_fusion.4
  1276.8 140.7 %collective-permute-done.1 = f32[1024,2048]{1,0:T(8,128)} collective-permute-done((f32[1024,2048]{1,0:T(8,128)}, f32[1024,2048]{1,0:T(8,128)}, u32[]{:S(2)}, u32[]{:S(2)}) %collective-permute-start.1) | collective-permute-done | bytes 8388640 | tf_op jit(solution)/shard_map/ppermute | solution.py:17
  1417.6 10.5 multiply_reduce_fusion
  1428.1 9.7 fusion.5
  1437.9 9.9 broadcast_multiply_fusion.4
  1455.5 11.6 fusion.18
  1480.2 13.8 fusion.78
  1510.9 9.4 fusion.12
  1526.6 9.2 multiply_reduce_fusion.7
  1586.5 10.2 pad.587
  1627.9 8.7 multiply_reduce_fusion.11
  1636.6 18.5 pad.589
  1659.2 12.1 pad.623
  1671.3 18.7 pad.624
  1690.0 12.1 pad.590
  1702.2 16.8 pad.568
  1718.9 10.9 pad.602
  1729.8 15.5 multiply_reduce_fusion.5
  1745.3 35.6 %pad.625 = f32[32,4,128,128]{2,3,1,0:T(8,128)} pad(f32[16,4,128,128]{2,3,1,0:T(8,128)} %get-tuple-element.256, f32[]{:T(128)} %constant.113.clone.1), padding=1_0_1x0_0_0x0_0_0x0_0_0 | pad | bytes 12582916 | tf_op jit(solution)/shard_map/transpose(jvp())/pad | solution.py:137
  1780.9 8.8 broadcast_multiply_fusion.1
  1789.7 35.6 %pad.591 = f32[32,4,128,128]{2,3,1,0:T(8,128)} pad(f32[16,4,128,128]{2,3,1,0:T(8,128)} %get-tuple-element.255, f32[]{:T(128)} %constant.113.clone.1), padding=1_0_1x0_0_0x0_0_0x0_0_0 | pad | bytes 12582916 | tf_op jit(solution)/shard_map/transpose(jvp())/pad | solution.py:137
  1825.3 35.7 %pad.592 = f32[32,4,128,128]{2,3,1,0:T(8,128)} pad(f32[16,4,128,128]{2,3,1,0:T(8,128)} %get-tuple-element.375, f32[]{:T(128)} %constant.113.clone.1), padding=0_1_1x0_0_0x0_0_0x0_0_0 | pad | bytes 12582916 | tf_op jit(solution)/shard_map/transpose(jvp())/pad | solution.py:137
  1861.0 33.8 %pad.562 = f32[32,4,128,128]{2,3,1,0:T(8,128)} pad(f32[15,4,128,128]{2,3,1,0:T(8,128)} %get-tuple-element.290, f32[]{:T(128)} %constant.113.clone.1), padding=2_1_1x0_0_0x0_0_0x0_0_0 | pad | bytes 12320772 | tf_op jit(solution)/shard_map/transpose(jvp())/pad | solution.py:137
  1894.8 9.9 add_add_fusion.3
  1904.8 8.6 fusion.103
  1913.4 15.1 fusion.83
  1931.9 35.7 %pad.626 = f32[32,4,128,128]{2,3,1,0:T(8,128)} pad(f32[16,4,128,128]{2,3,1,0:T(8,128)} %get-tuple-element.376, f32[]{:T(128)} %constant.113.clone.1), padding=0_1_1x0_0_0x0_0_0x0_0_0 | pad | bytes 12582916 | tf_op jit(solution)/shard_map/transpose(jvp())/pad | solution.py:137
  1967.6 33.6 %pad.597 = f32[32,4,128,128]{2,3,1,0:T(8,128)} pad(f32[15,4,128,128]{2,3,1,0:T(8,128)} %get-tuple-element.291, f32[]{:T(128)} %constant.113.clone.1), padding=2_1_1x0_0_0x0_0_0x0_0_0 | pad | bytes 12320772 | tf_op jit(solution)/shard_map/transpose(jvp())/pad | solution.py:137
  2001.3 10.2 add_add_fusion.2
  2018.9 14.6 fusion.176
  2040.3 15.1 fusion.81
  2060.2 7.9 fusion.111
  2068.2 14.0 fusion.41
  2093.9 12.6 convolution_convert_fusion.3
  2107.2 14.5 convolution_convert_fusion.2
  2129.7 147.7 %all-reduce.123.cloned.1.call-done = (bf16[1024,2048]{1,0:T(8,128)(2,1)}, bf16[1024,2048]{1,0:T(8,128)(2,1)}) async-done(((bf16[1024,2048]{1,0:T(8,128)(2,1)}, bf16[1024,2048]{1,0:T(8,128)(2,1)}), (bf16[1024,2048]{1,0:T(8,128)(2,1)}, bf16[1024,2048]{1,0:T(8,128)(2,1)})) %all-reduce.123.cloned.1.call-update) | async-done | bytes 8388624 | tf_op jit(solution)/shard_map/psum | solution.py:233
  2277.4 8.3 add_convert_fusion
  2285.7 84.9 %reduce-scatter.5.cloned.1.call-done = bf16[256,2048]{1,0:T(8,128)(2,1)} async-done(((bf16[2048,2048]{1,0:T(8,128)(2,1)}), bf16[256,2048]{1,0:T(8,128)(2,1)}) %reduce-scatter.5.cloned.1.call-update) | async-done | bytes 1048592 | tf_op jit(solution)/shard_map/reduce_scatter | solution.py:296
  2376.6 26.3 %all-reduce.116 = (bf16[2048]{0:T(1024)(128)(2,1)S(1)}, bf16[2048]{0:T(1024)(128)(2,1)S(1)}, bf16[512]{0:T(512)(128)(2,1)S(1)}, bf16[512]{0:T(512)(128)(2,1)S(1)}, bf16[24,512]{1,0:T(8,128)(2,1)S(1)}) all-reduce(bf16[2048]{0:T(1024)(128)(2,1)S(1)} %get-tuple-element.200, ...), channel_id=1, replica_groups=mesh['dp'=4,'ctx'=2,'tp'=4] {'dp','ctx'}, use_global_device_ids=true, to_apply=%region_50.51 | all-reduce | flops 17408 | bytes 69632 | tf_op jit(solution)/shard_map/psum | solution.py:324
  2405.9 9.5 fusion.6
  (747 shorter events, 350.7 us)
Async XLA Ops:
  7.2 155.7 %all-gather.8.cloned.1.call-start = ((), (), s32[]{:S(2)}) async-start(), calls=%async_computation.4 | async-start | bytes 10485760 | tf_op jit(solution)/shard_map/all_gather | solution.py:179
  10.4 477.5 %all-gather.10.cloned.1.call-start = ((), (), s32[]{:S(2)}) async-start(), calls=%async_computation.5 | async-start | bytes 2621440 | tf_op jit(solution)/shard_map/all_gather | solution.py:180
  11.1 654.8 %all-reduce.121.cloned.1.call-start = ((), (), s32[]{:S(2)}) async-start(), calls=%async_computation.6 | async-start | bytes 16777216 | tf_op jit(solution)/shard_map/psum | solution.py:221
  12.7 150.1 %copy-start.171 = (f32[2048]{0:T(1024)S(1)}, f32[2048]{0:T(1024)}, u32[]{:S(2)}) copy-start(f32[2048]{0:T(1024)} %param.28) | copy-start | bytes 24580
  16.4 159.0 %copy-start.161 = (f32[1024]{0:T(1024)}, f32[1024]{0:T(1024)S(1)}, u32[]{:S(2)}) copy-start(f32[1024]{0:T(1024)S(1)} %fusion.149) | copy-start | bytes 12292
  16.6 158.8 %copy-start.163 = (f32[512]{0:T(512)}, f32[512]{0:T(512)S(1)}, u32[]{:S(2)}) copy-start(f32[512]{0:T(512)S(1)} %multiply_reduce_fusion.28) | copy-start | bytes 6148
  16.6 158.8 %copy-start.178 = (f32[512]{0:T(512)}, f32[512]{0:T(512)S(1)}, u32[]{:S(2)}) copy-start(f32[512]{0:T(512)S(1)} %broadcast_subtract_fusion) | copy-start | bytes 6148
  16.7 169.3 %copy-start.196 = (f32[32]{0:T(128)}, f32[32]{0:T(128)S(1)}, u32[]{:S(2)}) copy-start(f32[32]{0:T(128)S(1)} %get-tuple-element.269) | copy-start | bytes 388
  16.9 1458.4 %copy-start.70 = (pred[32,32,32]{2,1,0:T(8,128)(4,1)}, pred[32,32,32]{2,1,0:T(8,128)(4,1)S(1)}, u32[]{:S(2)}) copy-start(pred[32,32,32]{2,1,0:T(8,128)(4,1)S(1)} %compare_and_fusion) | copy-start | bytes 98308
  16.9 189.2 %copy-start.126 = (f32[32,32]{0,1:T(8,128)}, f32[32,32]{0,1:T(8,128)S(1)}, u32[]{:S(2)}) copy-start(f32[32,32]{0,1:T(8,128)S(1)} %get-tuple-element.440) | copy-start | bytes 12292
  16.9 416.2 %copy-start.124 = (f32[32,32]{0,1:T(8,128)}, f32[32,32]{0,1:T(8,128)S(1)}, u32[]{:S(2)}) copy-start(f32[32,32]{0,1:T(8,128)S(1)} %get-tuple-element.439) | copy-start | bytes 12292
  17.0 158.5 %copy-start.186 = (f32[512]{0:T(512)S(1)}, f32[512]{0:T(512)}, u32[]{:S(2)}) copy-start(f32[512]{0:T(512)} %param.31) | copy-start | bytes 6148
  184.2 22.0 copy-start
  186.0 20.1 copy-start.103
  187.5 35.9 %copy-start.120 = (f32[16,4,128]{2,1,0:T(4,128)}, f32[16,4,128]{2,1,0:T(4,128)S(1)}, u32[]{:S(2)}) copy-start(f32[16,4,128]{2,1,0:T(4,128)S(1)} %get-tuple-element.356) | copy-start | bytes 98308
  187.5 39.5 %copy-start.135 = (f32[8,4,128]{2,1,0:T(4,128)}, f32[8,4,128]{2,1,0:T(4,128)S(1)}, u32[]{:S(2)}) copy-start(f32[8,4,128]{2,1,0:T(4,128)S(1)} %get-tuple-element.380) | copy-start | bytes 49156
  187.6 42.2 %copy-start.149 = (f32[4,4,128]{2,1,0:T(4,128)}, f32[4,4,128]{2,1,0:T(4,128)S(1)}, u32[]{:S(2)}) copy-start(f32[4,4,128]{2,1,0:T(4,128)S(1)} %get-tuple-element.402) | copy-start | bytes 24580
  187.6 42.3 %copy-start.156 = (f32[2,4,128]{2,1,0:T(4,128)}, f32[2,4,128]{2,1,0:T(4,128)S(1)}, u32[]{:S(2)}) copy-start(f32[2,4,128]{2,1,0:T(4,128)S(1)} %get-tuple-element.421) | copy-start | bytes 12292
  187.7 42.3 %copy-start.180 = (f32[4,128]{1,0:T(4,128)}, f32[4,128]{1,0:T(4,128)S(1)}, u32[]{:S(2)}) copy-start(f32[4,128]{1,0:T(4,128)S(1)} %get-tuple-element.431) | copy-start | bytes 6148
  229.0 16.9 copy-start.58
  268.2 18.7 copy-start.72
  347.5 35.8 %copy-start.188 = (f32[1,4,128]{2,1,0:T(4,128)S(1)}, f32[1,4,128]{2,1,0:T(4,128)}, u32[]{:S(2)}) copy-start(f32[1,4,128]{2,1,0:T(4,128)} %get-tuple-element.266) | copy-start | bytes 6148
  450.2 15.9 copy-start.52
  450.2 15.9 copy-start.99
  495.5 374.3 %all-gather.12.cloned.1.call-start = ((), (), s32[]{:S(2)}) async-start(), calls=%async_computation.7 | async-start | bytes 14417920 | tf_op jit(solution)/shard_map/all_gather | solution.py:224
  499.1 477.1 %all-gather.14.cloned.1.call-start = ((), (), s32[]{:S(2)}) async-start(), calls=%async_computation.8 | async-start | bytes 7208960 | tf_op jit(solution)/shard_map/all_gather | solution.py:225
  499.7 370.1 %copy-start.175 = (f32[2048]{0:T(1024)S(1)}, f32[2048]{0:T(1024)}, u32[]{:S(2)}) copy-start(f32[2048]{0:T(1024)} %param.29) | copy-start | bytes 24580
  499.7 777.0 %reduce-scatter.11.cloned.1.call-start = ((), (), s32[]{:S(2)}) async-start(), calls=%async_computation.14 | async-start | bytes 6488064 | tf_op jit(solution)/shard_map/reduce_scatter | solution.py:305
  976.2 18.5 copy-start.81
  1002.8 1119.0 %reduce-scatter.9.cloned.1.call-start = ((), (), s32[]{:S(2)}) async-start(), calls=%async_computation.12 | async-start | bytes 12976128 | tf_op jit(solution)/shard_map/reduce_scatter | solution.py:302
  1022.3 1100.2 %all-gather.20.cloned.1.call-start = ((), (), s32[]{:S(2)}) async-start(), calls=%async_computation.15 | async-start | bytes 2162688 | tf_op jit(solution)/shard_map/all_gather | solution.py:319
  1041.2 195.9 %copy-start.198 = (bf16[1,4,128]{2,1,0:T(4,128)(2,1)S(1)}, bf16[1,4,128]{2,1,0:T(4,128)(2,1)}, u32[]{:S(2)}) copy-start(bf16[1,4,128]{2,1,0:T(4,128)(2,1)} %get-tuple-element.265) | copy-start | bytes 3076
  1041.2 182.7 %collective-permute-start = (f32[1024,2048]{1,0:T(8,128)}, f32[1024,2048]{1,0:T(8,128)}, u32[]{:S(2)}, u32[]{:S(2)}) collective-permute-start(f32[1024,2048]{1,0:T(8,128)} %fusion.20), channel_id=1, source_target_pairs={{0,1},{1,0},{2,3},{3,2},{4,5},{5,4},{6,7},{7,6},{8,9},{9,8},{10,11... | collective-permute-start | bytes 25165832 | tf_op jit(solution)/shard_map/ppermute | solution.py:17
  1235.7 181.9 %collective-permute-start.1 = (f32[1024,2048]{1,0:T(8,128)}, f32[1024,2048]{1,0:T(8,128)}, u32[]{:S(2)}, u32[]{:S(2)}) collective-permute-start(f32[1024,2048]{1,0:T(8,128)} %add.608), channel_id=1, source_target_pairs={{0,2},{1,3},{2,0},{3,1},{4,6},{5,7},{6,4},{7,5},{8,10},{9,11},{10,... | collective-permute-start | bytes 25165832 | tf_op jit(solution)/shard_map/ppermute | solution.py:17
  1238.9 15.8 copy-start.57
  1276.8 849.4 %reduce-scatter.7.cloned.1.call-start = ((), (), s32[]{:S(2)}) async-start(), calls=%async_computation.11 | async-start | bytes 2359296 | tf_op jit(solution)/shard_map/reduce_scatter | solution.py:299
  1437.8 15.8 copy-start.112
  1455.5 24.7 %copy-start.25 = (f32[32,4,128,32]{2,3,1,0:T(8,128)}, f32[32,4,128,32]{2,3,1,0:T(8,128)S(1)}, u32[]{:S(2)}) copy-start(f32[32,4,128,32]{2,3,1,0:T(8,128)S(1)} %fusion.21) | copy-start | bytes 6291460
  1636.6 18.5 copy-start.136
  1671.3 18.7 copy-start.77
  1702.2 16.8 copy-start.78
  1745.3 35.7 %copy-start.121 = (f32[16,4,128]{2,1,0:T(4,128)S(1)}, f32[16,4,128]{2,1,0:T(4,128)}, u32[]{:S(2)}) copy-start(f32[16,4,128]{2,1,0:T(4,128)} %copy-done.120) | copy-start | bytes 98308
  1861.0 33.8 %slice-start.6 = ((f32[16,4,128,128]{2,3,1,0:T(8,128)}), f32[1,4,128,128]{2,3,1,0:T(8,128)S(1)}, s32[]{:S(2)}) async-start(f32[16,4,128,128]{2,3,1,0:T(8,128)} %slice.453), calls=%async_computation.23 | async-start | bytes 524288 | tf_op jit(solution)/shard_map/transpose(jvp())/split | solution.py:137
  1913.3 15.5 copy-start.141
  1913.3 15.5 copy-start.142
  1913.4 16.0 copy-start.115
  1913.4 16.0 copy-start.132
  1913.4 16.0 copy-start.134
  1913.4 16.0 copy-start.151
  1928.7 38.9 %copy-start.137 = (f32[16,4,128]{2,1,0:T(4,128)}, f32[16,4,128]{2,1,0:T(4,128)S(1)}, u32[]{:S(2)}) copy-start(f32[16,4,128]{2,1,0:T(4,128)S(1)} %slice.469) | copy-start | bytes 98308
  1928.7 38.8 %copy-start.138 = (f32[16,4,128]{2,1,0:T(4,128)}, f32[16,4,128]{2,1,0:T(4,128)S(1)}, u32[]{:S(2)}) copy-start(f32[16,4,128]{2,1,0:T(4,128)S(1)} %slice.477) | copy-start | bytes 98308
  1967.6 33.6 %slice-start.7 = ((f32[16,4,128,128]{2,3,1,0:T(8,128)}), f32[1,4,128,128]{2,3,1,0:T(8,128)S(1)}, s32[]{:S(2)}) async-start(f32[16,4,128,128]{2,3,1,0:T(8,128)} %copy-done.61), calls=%async_computation.24 | async-start | bytes 524288 | tf_op jit(solution)/shard_map/transpose(jvp())/split | solution.py:137
  2001.2 17.5 copy-start.100
  2001.2 17.5 copy-start.104
  2001.2 17.5 copy-start.125
  2001.3 17.5 copy-start.127
  2018.9 15.7 copy-start.53
  2034.6 20.9 slice-start.1
  2037.1 18.4 slice-start.2
  2059.3 218.1 %all-reduce.123.cloned.1.call-start = ((), (), s32[]{:S(2)}) async-start(), calls=%async_computation.16 | async-start | bytes 16777216 | tf_op jit(solution)/shard_map/psum | solution.py:233
  2106.5 264.1 %reduce-scatter.5.cloned.1.call-start = ((), (), s32[]{:S(2)}) async-start(), calls=%async_computation.9 | async-start | bytes 9437184 | tf_op jit(solution)/shard_map/reduce_scatter | solution.py:296
  2121.7 293.7 %all-gather.18.cloned.1.call-start = ((), (), s32[]{:S(2)}) async-start(), calls=%async_computation.13 | async-start | bytes 4325376 | tf_op jit(solution)/shard_map/all_gather | solution.py:316
  2122.3 297.8 %all-gather.16.cloned.1.call-start = ((), (), s32[]{:S(2)}) async-start(), calls=%async_computation.10 | async-start | bytes 3145728 | tf_op jit(solution)/shard_map/all_gather | solution.py:310
  2370.6 35.2 %copy-start.158 = (f32[1024]{0:T(1024)S(1)}, f32[1024]{0:T(1024)}, u32[]{:S(2)}) copy-start(f32[1024]{0:T(1024)} %copy-done.157) | copy-start | bytes 12292
  (173 other events, 868.3 us)
Sparse Core Ops, SparseCore 0:
  10.5 152.3 all-gather.7
  164.4 44.1 all-gather.9
  495.6 170.3 all-reduce.120
  668.0 201.7 all-gather.11
  871.3 104.8 all-gather.13
  1002.9 63.0 reduce-scatter.10
  1068.5 117.6 reduce-scatter.8
  1276.9 6.7 all-gather.19
  2059.4 33.9 reduce-scatter.6
  2106.7 170.6 all-reduce.122
  2280.3 90.2 reduce-scatter.4
  2372.0 10.0 all-gather.17
  2383.7 11.7 all-gather.15
